TPU v7x, 32 devices: a whole 2x2x4 slice. The times are simulated.
32 devices in a mesh: energy: 16 (over z, y, x), slab: 2 (over core).
Axes of the slice: x: 2, y: 2, z: 4, core: 2. Of those that a mesh axis runs over, the one named last changes fastest.
Arguments:
- green0: bfloat16 [16, 2, 2, 384, 384], P('energy', 'slab'), may hold values from -6 to 6
- coupling: bfloat16 [2, 3, 384, 384], P('slab'), may hold values from -0.09375 to 0.09375
Outputs:
- green: bfloat16 [16, 2, 2, 384, 384], P('energy', 'slab')
All inputs are finite; a program needn't handle non-finite values.
Results may differ from a plain program's by a relative error of at most 0.012.
Values may be sent and summed in bfloat16 or wider, within the bound.
No kernel may reach another device: no remote copies, remote signals or barrier semaphores. Data moves between devices by JAX's collectives and lax.ppermute only.
A program may use at most 64 MiB of HBM per device.

v0:
```python
import functools

import jax
import jax.numpy as jnp
from jax import lax
from jax.experimental import pallas as pl
from jax.experimental.pallas import tpu as pltpu
from jax.sharding import PartitionSpec as P

OFFSET = 7
ITERS = 2
VMEM_LIMIT = 12 << 20
ROW, LAYER = 2, 4


def passed_along(value, axis, steps):
    count = lax.axis_size(axis)
    first, last = (max(0, -steps), min(count, count - steps))
    return lax.ppermute(value, axis, [(source, source + steps) for source in range(first, last)])


def with_halo(block, sides, width):
    for axis, dim in sides:
        count = lax.axis_size(axis)
        forward = [(i, i + 1) for i in range(count - 1)]
        backward = [(target, source) for source, target in forward]
        low = lax.ppermute(
            lax.slice_in_dim(block, block.shape[dim] - width, None, axis=dim), axis, forward
        )
        high = lax.ppermute(lax.slice_in_dim(block, 0, width, axis=dim), axis, backward)
        block = jnp.concatenate([low, block, high], axis=dim)
    return block


def dyson(green0, coupling, summed):
    count = green0.shape[1]
    size = green0.shape[-1]
    sigma = jnp.zeros(green0.shape, jnp.float32)
    for index in range(3):
        part = summed[:, index : index + count]
        weights = coupling[:, index]
        left = jnp.einsum(
            "sij,escjk->escik", weights, part, preferred_element_type=jnp.float32
        ).astype(jnp.bfloat16)
        sigma = sigma + jnp.einsum(
            "escij,skj->escik", left, weights, preferred_element_type=jnp.float32
        )
    sigma = sigma.astype(jnp.bfloat16)
    green_re = green0[:, :, 0]
    green_im = green0[:, :, 1]
    form = "esij,esjk->esik"
    prod_re = jnp.einsum(
        form, green_re, sigma[:, :, 0], preferred_element_type=jnp.float32
    ) - jnp.einsum(form, green_im, sigma[:, :, 1], preferred_element_type=jnp.float32)
    prod_im = jnp.einsum(
        form, green_re, sigma[:, :, 1], preferred_element_type=jnp.float32
    ) + jnp.einsum(form, green_im, sigma[:, :, 0], preferred_element_type=jnp.float32)
    prod_re = prod_re.astype(jnp.bfloat16)
    prod_im = prod_im.astype(jnp.bfloat16)
    trans = "esij,eskj->esik"
    out_re = jnp.einsum(trans, prod_re, green_re, preferred_element_type=jnp.float32) - jnp.einsum(
        trans, prod_im, green_im, preferred_element_type=jnp.float32
    )
    out_im = jnp.einsum(trans, prod_re, green_im, preferred_element_type=jnp.float32) + jnp.einsum(
        trans, prod_im, green_re, preferred_element_type=jnp.float32
    )
    result = green0.astype(jnp.float32) + jnp.stack([out_re, out_im], axis=2) / size
    return result.astype(jnp.bfloat16)


def plain(green0, coupling):
    green = green0
    for _ in range(ITERS):
        lower = passed_along(green, "energy", OFFSET)
        upper = passed_along(green, "energy", -OFFSET)
        own_sum = (lower.astype(jnp.float32) + upper.astype(jnp.float32)).astype(jnp.bfloat16)
        summed = with_halo(own_sum, (("slab", 1),), 1)
        green = dyson(green0, coupling, summed)
    return green


def links(source, target):
    passed, at = [], source
    for step, size in ((LAYER, None), (1, ROW), (ROW, LAYER)):
        here, there = ((e // step if size is None else e % size // step) for e in (at, target))
        for _ in range(abs(there - here)):
            to = at + (step if there > here else -step)
            passed.append((at, to))
            at = to
    return passed


def planned(energies):
    chains = [list(range(first, energies, OFFSET)) for first in range(min(OFFSET, energies))]
    threes = [chain for chain in chains if len(chain) == 3]
    twos = [chain for chain in chains if len(chain) == 2]
    if len(threes) != 2 or len(threes) + len(twos) != len(chains):
        return None
    (low0, mid0, high0), (low1, mid1, high1) = threes
    inward = [(low0, mid0), (low1, mid1), (high0, mid0), (high1, mid1)]
    plan = {
        "first": inward[:2],
        "other": inward[2:],
        "second": [(mid0, low0), (mid1, low1)],
        "third": [(mid0, high0), (mid1, high1)],
    }
    busy = {link for flow in inward for link in links(*flow)}
    taken = set()
    direct, late, relays = [], [], []
    for source, target in [flow for a, b in twos for flow in ((a, b), (b, a))]:
        passed = set(links(source, target))
        relay = target - target % LAYER + source % LAYER
        if passed & taken or any(abs(a - b) == LAYER for a, b in passed & busy):
            plan["second"].append((source, target))
            late.append((source, target))
        elif passed & busy:
            plan["other"].append((source, relay))
            plan["second"].append((relay, target))
            relays.append((relay, target))
            taken |= set(links(source, relay))
        else:
            plan["first"].append((source, target))
            direct.append(target)
            taken |= passed
    for flows in plan.values():
        sources, targets = zip(*flows)
        if len(set(sources)) < len(flows) or len(set(targets)) < len(flows):
            return None
    plan["lows"], plan["mids"], plan["highs"] = ([a, b] for a, b in zip(*threes))
    plan["direct"] = direct
    plan["relayed"] = [relay for relay, _ in relays]
    plan["late"] = [source for source, _ in late]
    plan["second_pairs"] = [target for _, target in late + relays]
    return plan


def dot(left, right):
    return jnp.dot(left, right, preferred_element_type=jnp.float32)


def dot_t(left, right):
    return lax.dot_general(
        left, right, (((1,), (1,)), ((), ())), preferred_element_type=jnp.float32
    )


def among(members):
    energy = lax.axis_index("energy")
    return functools.reduce(jnp.logical_or, [energy == member for member in members])


def half_energy(block, weight):
    size = block.shape[-1]
    left = dot(weight, jnp.concatenate([block[0], block[1]], axis=1)).astype(jnp.bfloat16)
    return dot_t(jnp.concatenate([left[:, :size], left[:, size:]], axis=0), weight)


def far_weight(weights):
    return weights[2 - 2 * lax.axis_index("slab")]


def self_energy(mine, other, weights):
    size = mine.shape[-1]
    own, far = weights[1], far_weight(weights)
    near = dot(own, jnp.concatenate([mine[0], mine[1]], axis=1)).astype(jnp.bfloat16)
    cross = dot(far, jnp.concatenate([other[0], other[1]], axis=1)).astype(jnp.bfloat16)
    left = jnp.concatenate(
        [
            jnp.concatenate([near[:, :size], cross[:, :size]], axis=1),
            jnp.concatenate([near[:, size:], cross[:, size:]], axis=1),
        ],
        axis=0,
    )
    return dot_t(left, jnp.concatenate([own, far], axis=1)).astype(jnp.bfloat16)


def stepped(green, sigma_re, sigma_im):
    re, im = green[0], green[1]
    size = re.shape[0]
    square = jnp.concatenate(
        [
            jnp.concatenate([sigma_re, sigma_im], axis=1),
            jnp.concatenate([-sigma_im, sigma_re], axis=1),
        ],
        axis=0,
    )
    product = dot(jnp.concatenate([re, im], axis=1), square).astype(jnp.bfloat16)
    turned = jnp.concatenate(
        [jnp.concatenate([re, -im], axis=1), jnp.concatenate([im, re], axis=1)], axis=0
    )
    added = dot_t(product, turned)
    return (
        re.astype(jnp.float32) + added[:, :size] / size,
        im.astype(jnp.float32) + added[:, size:] / size,
    )


def put(out, parts):
    for part, value in enumerate(parts):
        out[part] = value.astype(out.dtype)


def added(one, two):
    return (one.astype(jnp.float32) + two.astype(jnp.float32)).astype(one.dtype)


def load_kernel(own, weights, own_out, weights_out, sems):
    copies = [
        pltpu.make_async_copy(own, own_out, sems.at[0]),
        pltpu.make_async_copy(weights, weights_out, sems.at[1]),
    ]
    for copy in copies:
        copy.start()
    for copy in copies:
        copy.wait()


def sigma_kernel(plan, own, beside, weights, out):
    size = own.shape[-1]

    @pl.when(jnp.logical_not(among(plan["lows"] + plan["highs"])))
    def _():
        sigma = self_energy(own, beside, weights)
        out[0] = sigma[:size]
        out[1] = sigma[size:]


def sum_kernel(plan, first, other, out):
    @pl.when(among(plan["mids"]))
    def _():
        out[...] = added(first[...], other[...])


def near_kernel(plan, both, weights, out):
    @pl.when(among(plan["mids"]))
    def _():
        out[...] = half_energy(both, weights[1])


def second_kernel(plan, own, near, across, weights, other, send):
    @pl.when(among(plan["mids"]))
    def _():
        size = own.shape[-1]
        sigma = near[...] + half_energy(across, far_weight(weights))
        sigma = sigma.astype(jnp.bfloat16)
        put(send, stepped(own, sigma[:size], sigma[size:]))

    for members, source in ((plan["relayed"], other), (plan["late"], own)):

        @pl.when(among(members))
        def _():
            send[...] = source[...]


def middle_kernel(plan, first, other, sigma, out):
    @pl.when(among(plan["mids"]))
    def _():
        steps = [stepped(block, sigma[0], sigma[1]) for block in (first, other)]
        put(out, [added(*(step[part].astype(out.dtype) for step in steps)) for part in range(2)])


def neighbour_kernel(plan, first, second, third, middle, sigma, out):
    for members, source in ((plan["direct"], first), (plan["second_pairs"], second)):

        @pl.when(among(members))
        def _():
            put(out, stepped(source, sigma[0], sigma[1]))

    for members, source in (
        (plan["lows"], second),
        (plan["mids"], middle),
        (plan["highs"], third),
    ):

        @pl.when(among(members))
        def _():
            out[...] = source[...]


def close_kernel(plan, green, weights, out):
    out[...] = half_energy(green, weights[1])


def last_kernel(plan, own, near, across, weights, out):
    size = own.shape[-1]
    sigma = near[...] + half_energy(across, far_weight(weights))
    sigma = sigma.astype(jnp.bfloat16)
    put(out, stepped(own, sigma[:size], sigma[size:]))


LIMITS = pltpu.CompilerParams(vmem_limit_bytes=VMEM_LIMIT)
IN_VMEM = pl.BlockSpec(memory_space=pltpu.VMEM)
IN_HBM = pl.BlockSpec(memory_space=pltpu.HBM)


def like(block, space=jax.ShapeDtypeStruct):
    return space(block.shape, block.dtype)


def call(kernel, plan, *blocks, out=None):
    return pl.pallas_call(
        functools.partial(kernel, plan),
        out_shape=out or like(blocks[0]),
        in_specs=[IN_VMEM] * len(blocks),
        out_specs=IN_VMEM,
        compiler_params=LIMITS,
    )(*blocks)


def loaded(own, weights):
    return pl.pallas_call(
        load_kernel,
        out_shape=[like(own), like(weights)],
        in_specs=[IN_HBM] * 2,
        out_specs=[IN_VMEM] * 2,
        scratch_shapes=[pltpu.SemaphoreType.DMA((2,))],
        compiler_params=LIMITS,
        name="load_kernel",
    )(own, weights)


def chained(plan, green0, coupling):
    slabs = lax.axis_size("slab")
    everyone = range(lax.axis_size("energy"))
    size = green0.shape[-1]
    wide = jax.ShapeDtypeStruct((2 * size, size), jnp.float32)

    def sent(value, flows):
        return lax.ppermute(value, "energy", plan[flows])

    def swapped(value, members):
        flows = [(e * slabs + s, e * slabs + slabs - 1 - s) for e in members for s in range(slabs)]
        return lax.ppermute(value, ("energy", "slab"), flows)

    far = pltpu.with_memory_space_constraint(green0[0, 0], pltpu.HBM)
    far_weights = pltpu.with_memory_space_constraint(coupling[0], pltpu.HBM)
    first, other = sent(green0[0, 0], "first"), sent(green0[0, 0], "other")
    own, weights = loaded(far, far_weights)
    sigma = call(sigma_kernel, plan, own, swapped(own, everyone), weights)
    both = call(sum_kernel, plan, first, other)
    across = swapped(both, everyone)
    near = call(near_kernel, plan, both, weights, out=wide)
    send = call(second_kernel, plan, own, near, across, weights, other)
    second, third = sent(send, "second"), sent(send, "third")
    middle = call(middle_kernel, plan, first, other, sigma)
    green = call(neighbour_kernel, plan, first, second, third, middle, sigma)
    across = swapped(green, everyone)
    near = call(close_kernel, plan, green, weights, out=wide)
    out = call(last_kernel, plan, own, near, across, weights)
    return out[None, None]


def solution(mesh):
    plan = planned(mesh.shape["energy"]) if mesh.shape["slab"] == 2 else None
    local = functools.partial(chained, plan) if plan else plain
    placed = (P("energy", "slab", None, None, None), P("slab", None, None, None))
    return jax.shard_map(
        local,
        mesh=mesh,
        in_specs=placed,
        out_specs=P("energy", "slab", None, None, None),
        check_vma=False,
    )
```

profile of v0, /device:TPU:0, one launch (start us, length us, event | category | flops | bytes accessed | tf_op | source)
XLA Modules:
  0.0 51.1 jit_solution(12833049696739366773)
XLA Ops:
  0.0 0.7 %collective-permute-start.1 = (bf16[2,384,384]{2,1,0:T(8,128)(2,1)}, bf16[2,384,384]{2,1,0:T(8,128)(2,1)S(1)}, u32[]{:S(2)}, u32[]{:S(2)}) collective-permute-start(bf16[2,384,384]{2,1,0:T(8,128)(2,1)} %bitcast.4), channel_id=1, source_target_pairs={{28,14},{30,16},{6,22},{24,8},{29,15},{31,17},{7,23},{25,9}} | collective-permute-start | bytes 1769480 | tf_op jit(solution)/shard_map/ppermute | solution.py:329
  0.7 7.5 %collective-permute-start = (bf16[2,384,384]{2,1,0:T(8,128)(2,1)}, bf16[2,384,384]{2,1,0:T(8,128)(2,1)S(1)}, u32[]{:S(2)}, u32[]{:S(2)}) collective-permute-start(bf16[2,384,384]{2,1,0:T(8,128)(2,1)} %bitcast.5), channel_id=1, source_target_pairs={{0,14},{2,16},{4,18},{18,4},{8,22},{22,8},{1,15},{3,17},{5,19},{19... | collective-permute-start | bytes 1769480 | tf_op jit(solution)/shard_map/ppermute | solution.py:329
  8.2 0.0 collective-permute-done.1.other
  8.2 12.8 %collective-permute-done.first = bf16[2,384,384]{2,1,0:T(8,128)(2,1)S(1)} collective-permute-done((bf16[2,384,384]{2,1,0:T(8,128)(2,1)}, bf16[2,384,384]{2,1,0:T(8,128)(2,1)S(1)}, u32[]{:S(2)}, u32[]{:S(2)}) %collective-permute-start) | collective-permute-done | bytes 589856 | tf_op jit(solution)/shard_map/ppermute | solution.py:329
  21.0 0.0 collective-permute-start.2
  21.0 1.4 %load_kernel.1 = (bf16[2,384,384]{2,1,0:T(8,128)(2,1)S(1)}, bf16[3,384,384]{2,1,0:T(8,128)(2,1)S(1)}) custom-call(bf16[2,384,384]{2,1,0:T(8,128)(2,1)} %bitcast.6, bf16[3,384,384]{2,1,0:T(8,128)(2,1)} %bitcast.3), custom_call_target="tpu_custom_call" | custom-call | tf_op jit(solution)/shard_map/load_kernel/pallas_call | solution.py:311
  22.4 0.6 %collective-permute-start.5 = (bf16[2,384,384]{2,1,0:T(8,128)(2,1)S(1)}, bf16[2,384,384]{2,1,0:T(8,128)(2,1)S(1)}, u32[]{:S(2)}, u32[]{:S(2)}) collective-permute-start(bf16[2,384,384]{2,1,0:T(8,128)(2,1)S(1)} %get-tuple-element.7.own), channel_id=1, source_target_pairs={{0,1},{1,0},{2,3},{3,2},{4,5},{5,4},{6,7},{7,6},{8,9},{9,8},{10,11... | collective-permute-start | bytes 1769480 | tf_op jit(solution)/shard_map/ppermute | solution.py:333
  23.0 0.1 collective-permute-done.2.across
  23.0 0.7 %collective-permute-start.4 = (bf16[2,384,384]{2,1,0:T(8,128)(2,1)S(1)}, bf16[2,384,384]{2,1,0:T(8,128)(2,1)S(1)}, u32[]{:S(2)}, u32[]{:S(2)}) collective-permute-start(bf16[2,384,384]{2,1,0:T(8,128)(2,1)S(1)} %shard_map.30), channel_id=1, source_target_pairs={{14,28},{16,30},{15,29},{17,31}} | collective-permute-start | bytes 1769480 | tf_op jit(solution)/shard_map/ppermute | solution.py:329
  23.7 1.3 %collective-permute-start.3 = (bf16[2,384,384]{2,1,0:T(8,128)(2,1)S(1)}, bf16[2,384,384]{2,1,0:T(8,128)(2,1)S(1)}, u32[]{:S(2)}, u32[]{:S(2)}) collective-permute-start(bf16[2,384,384]{2,1,0:T(8,128)(2,1)S(1)} %shard_map.30), channel_id=1, source_target_pairs={{14,0},{16,2},{22,20},{20,6},{10,24},{8,10},{12,26},{26,12},{15,1}... | collective-permute-start | bytes 1769480 | tf_op jit(solution)/shard_map/ppermute | solution.py:329
  25.0 0.0 collective-permute-done.5.beside
  25.1 0.0 collective-permute-done.4.third
  25.1 21.1 %collective-permute-done.3.second = bf16[2,384,384]{2,1,0:T(8,128)(2,1)S(1)} collective-permute-done((bf16[2,384,384]{2,1,0:T(8,128)(2,1)S(1)}, bf16[2,384,384]{2,1,0:T(8,128)(2,1)S(1)}, u32[]{:S(2)}, u32[]{:S(2)}) %collective-permute-start.3) | collective-permute-done | bytes 589856 | tf_op jit(solution)/shard_map/ppermute | solution.py:329
  46.2 0.1 shard_map.33.green
  46.3 0.1 collective-permute-start.6
  46.4 0.8 %shard_map.34.near = f32[768,384]{1,0:T(8,128)S(1)} custom-call(bf16[2,384,384]{2,1,0:T(8,128)(2,1)S(1)} %shard_map.33.green, bf16[3,384,384]{2,1,0:T(8,128)(2,1)S(1)} %get-tuple-element.8.weights), custom_call_target="tpu_custom_call" | custom-call | tf_op jit(solution)/shard_map/pallas_call | solution.py:301
  47.2 1.2 %collective-permute-done.6.across = bf16[2,384,384]{2,1,0:T(8,128)(2,1)S(1)} collective-permute-done((bf16[2,384,384]{2,1,0:T(8,128)(2,1)S(1)}, bf16[2,384,384]{2,1,0:T(8,128)(2,1)S(1)}, u32[]{:S(2)}, u32[]{:S(2)}) %collective-permute-start.6) | collective-permute-done | bytes 589856 | tf_op jit(solution)/shard_map/ppermute | solution.py:333
  48.4 2.7 %shard_map.35 = bf16[2,384,384]{2,1,0:T(8,128)(2,1)} custom-call(bf16[2,384,384]{2,1,0:T(8,128)(2,1)S(1)} %get-tuple-element.7.own, f32[768,384]{1,0:T(8,128)S(1)} %shard_map.34.near, bf16[2,384,384]{2,1,0:T(8,128)(2,1)S(1)} %collective-permute-done.6.across, bf16[3,384,384]{2,1,0:T(8,128)(2,1)S(1)} %get-tuple-element.8.weights), custom_call_target="tpu_custom_call" | custom-call | tf_op jit(solution)/shard_map/pallas_call | solution.py:301
  (5 shorter events, 0.0 us)
Async XLA Ops:
  0.0 8.2 %collective-permute-start.1 = (bf16[2,384,384]{2,1,0:T(8,128)(2,1)}, bf16[2,384,384]{2,1,0:T(8,128)(2,1)S(1)}, u32[]{:S(2)}, u32[]{:S(2)}) collective-permute-start(bf16[2,384,384]{2,1,0:T(8,128)(2,1)} %bitcast.4), channel_id=1, source_target_pairs={{28,14},{30,16},{6,22},{24,8},{29,15},{31,17},{7,23},{25,9}} | collective-permute-start | bytes 1769480 | tf_op jit(solution)/shard_map/ppermute | solution.py:329
  0.7 20.3 %collective-permute-start = (bf16[2,384,384]{2,1,0:T(8,128)(2,1)}, bf16[2,384,384]{2,1,0:T(8,128)(2,1)S(1)}, u32[]{:S(2)}, u32[]{:S(2)}) collective-permute-start(bf16[2,384,384]{2,1,0:T(8,128)(2,1)} %bitcast.5), channel_id=1, source_target_pairs={{0,14},{2,16},{4,18},{18,4},{8,22},{22,8},{1,15},{3,17},{5,19},{19... | collective-permute-start | bytes 1769480 | tf_op jit(solution)/shard_map/ppermute | solution.py:329
  21.0 2.0 %collective-permute-start.2 = (bf16[2,384,384]{2,1,0:T(8,128)(2,1)S(1)}, bf16[2,384,384]{2,1,0:T(8,128)(2,1)S(1)}, u32[]{:S(2)}, u32[]{:S(2)}) collective-permute-start(bf16[2,384,384]{2,1,0:T(8,128)(2,1)S(1)} %shard_map.28.both), channel_id=1, source_target_pairs={{0,1},{1,0},{2,3},{3,2},{4,5},{5,4},{6,7},{7,6},{8,9},{9,8},{10,11... | collective-permute-start | bytes 1769480 | tf_op jit(solution)/shard_map/ppermute | solution.py:333
  22.4 2.6 %collective-permute-start.5 = (bf16[2,384,384]{2,1,0:T(8,128)(2,1)S(1)}, bf16[2,384,384]{2,1,0:T(8,128)(2,1)S(1)}, u32[]{:S(2)}, u32[]{:S(2)}) collective-permute-start(bf16[2,384,384]{2,1,0:T(8,128)(2,1)S(1)} %get-tuple-element.7.own), channel_id=1, source_target_pairs={{0,1},{1,0},{2,3},{3,2},{4,5},{5,4},{6,7},{7,6},{8,9},{9,8},{10,11... | collective-permute-start | bytes 1769480 | tf_op jit(solution)/shard_map/ppermute | solution.py:333
  23.0 2.1 %collective-permute-start.4 = (bf16[2,384,384]{2,1,0:T(8,128)(2,1)S(1)}, bf16[2,384,384]{2,1,0:T(8,128)(2,1)S(1)}, u32[]{:S(2)}, u32[]{:S(2)}) collective-permute-start(bf16[2,384,384]{2,1,0:T(8,128)(2,1)S(1)} %shard_map.30), channel_id=1, source_target_pairs={{14,28},{16,30},{15,29},{17,31}} | collective-permute-start | bytes 1769480 | tf_op jit(solution)/shard_map/ppermute | solution.py:329
  23.7 22.5 %collective-permute-start.3 = (bf16[2,384,384]{2,1,0:T(8,128)(2,1)S(1)}, bf16[2,384,384]{2,1,0:T(8,128)(2,1)S(1)}, u32[]{:S(2)}, u32[]{:S(2)}) collective-permute-start(bf16[2,384,384]{2,1,0:T(8,128)(2,1)S(1)} %shard_map.30), channel_id=1, source_target_pairs={{14,0},{16,2},{22,20},{20,6},{10,24},{8,10},{12,26},{26,12},{15,1}... | collective-permute-start | bytes 1769480 | tf_op jit(solution)/shard_map/ppermute | solution.py:329
  46.3 2.1 %collective-permute-start.6 = (bf16[2,384,384]{2,1,0:T(8,128)(2,1)S(1)}, bf16[2,384,384]{2,1,0:T(8,128)(2,1)S(1)}, u32[]{:S(2)}, u32[]{:S(2)}) collective-permute-start(bf16[2,384,384]{2,1,0:T(8,128)(2,1)S(1)} %shard_map.33.green), channel_id=1, source_target_pairs={{0,1},{1,0},{2,3},{3,2},{4,5},{5,4},{6,7},{7,6},{8,9},{9,8},{10,11... | collective-permute-start | bytes 1769480 | tf_op jit(solution)/shard_map/ppermute | solution.py:333
where the time goes:
time: 51.2 us; the launch traced here: 51.1 us
  waiting for transfers between devices  35.2 us (69%)
  starting transfers between devices  10.8 us (21%)
  Pallas kernels  4.97 us (10%)
    ppermute x4, waiting for transfers between devices, sent(): return lax.ppermute(value, 'energy', plan[flows])  34 us
    ppermute x4, starting transfers between devices, sent(): return lax.ppermute(value, 'energy', plan[flows])  10.1 us
    pallas_call x8, Pallas kernels, call(): pl.pallas_call(functools.partial(kernel, plan), out_shape=out or like(blo...  3.61 us
    pallas_call x1, Pallas kernels, loaded(): pl.pallas_call(load_kernel, out_shape=[like(own), like(weights)], in_spec...  1.37 us
    ppermute x3, waiting for transfers between devices, swapped(): return lax.ppermute(value, ('energy', 'slab'), flows)  1.22 us
  transfers between devices with their start and end apart: 7, of which 4 were waited for; matrix products, arithmetic and copies ran while one was open for 0% of the time, Pallas kernels for 4%

commit v1 on v0

--- a/solution.py
+++ b/solution.py
@@ -114,20 +114,23 @@
             plan["second"].append((source, target))
             late.append((source, target))
         elif passed & busy:
-            plan["other"].append((source, relay))
+            plan["first"].append((source, relay))
             plan["second"].append((relay, target))
             relays.append((relay, target))
             taken |= set(links(source, relay))
         else:
-            plan["first"].append((source, target))
-            direct.append(target)
+            direct.append((source, target))
             taken |= passed
+    relayed = {relay for relay, _ in relays}
+    plan["first"] += [flow for flow in direct if flow[1] not in relayed]
+    plan["other"] += [flow for flow in direct if flow[1] in relayed]
     for flows in plan.values():
         sources, targets = zip(*flows)
         if len(set(sources)) < len(flows) or len(set(targets)) < len(flows):
             return None
     plan["lows"], plan["mids"], plan["highs"] = ([a, b] for a, b in zip(*threes))
-    plan["direct"] = direct
+    plan["direct"] = [target for _, target in direct if target in relayed]
+    plan["early"] = [target for _, target in direct if target not in relayed]
     plan["relayed"] = [relay for relay, _ in relays]
     plan["late"] = [source for source, _ in late]
     plan["second_pairs"] = [target for _, target in late + relays]
@@ -147,12 +150,6 @@
 def among(members):
     energy = lax.axis_index("energy")
     return functools.reduce(jnp.logical_or, [energy == member for member in members])
-
-
-def half_energy(block, weight):
-    size = block.shape[-1]
-    left = dot(weight, jnp.concatenate([block[0], block[1]], axis=1)).astype(jnp.bfloat16)
-    return dot_t(jnp.concatenate([left[:, :size], left[:, size:]], axis=0), weight)
 
 
 def far_weight(weights):
@@ -174,13 +171,11 @@
     return dot_t(left, jnp.concatenate([own, far], axis=1)).astype(jnp.bfloat16)
 
 
-def stepped(green, sigma_re, sigma_im):
-    re, im = green[0], green[1]
-    size = re.shape[0]
+def around(re, im, block_re, block_im):
     square = jnp.concatenate(
         [
-            jnp.concatenate([sigma_re, sigma_im], axis=1),
-            jnp.concatenate([-sigma_im, sigma_re], axis=1),
+            jnp.concatenate([block_re, block_im], axis=1),
+            jnp.concatenate([-block_im, block_re], axis=1),
         ],
         axis=0,
     )
@@ -188,11 +183,19 @@
     turned = jnp.concatenate(
         [jnp.concatenate([re, -im], axis=1), jnp.concatenate([im, re], axis=1)], axis=0
     )
-    added = dot_t(product, turned)
-    return (
-        re.astype(jnp.float32) + added[:, :size] / size,
-        im.astype(jnp.float32) + added[:, size:] / size,
-    )
+    return dot_t(product, turned)
+
+
+def onto(green, added):
+    size = added.shape[0]
+    return [
+        green[part].astype(jnp.float32) + added[:, part * size : (part + 1) * size] / size
+        for part in range(2)
+    ]
+
+
+def stepped(green, sigma):
+    return onto(green, around(green[0], green[1], sigma[0], sigma[1]))
 
 
 def put(out, parts):
@@ -231,21 +234,27 @@
         out[...] = added(first[...], other[...])
 
 
-def near_kernel(plan, both, weights, out):
+def turn_kernel(plan, own, weights, near, far):
+    size = own.shape[-1]
+    both = jnp.concatenate([weights[1], far_weight(weights)], axis=1)
+    for part in range(2):
+        turn = dot(own[part], both).astype(jnp.bfloat16)
+        near[part] = turn[:, :size]
+        far[part] = turn[:, size:]
+
+
+def near_kernel(plan, turn, both, out):
     @pl.when(among(plan["mids"]))
     def _():
-        out[...] = half_energy(both, weights[1])
-
-
-def second_kernel(plan, own, near, across, weights, other, send):
+        out[...] = around(turn[0], turn[1], both[0], both[1])
+
+
+def second_kernel(plan, own, turn, near, across, first, send):
     @pl.when(among(plan["mids"]))
     def _():
-        size = own.shape[-1]
-        sigma = near[...] + half_energy(across, far_weight(weights))
-        sigma = sigma.astype(jnp.bfloat16)
-        put(send, stepped(own, sigma[:size], sigma[size:]))
-
-    for members, source in ((plan["relayed"], other), (plan["late"], own)):
+        put(send, onto(own, near[...] + around(turn[0], turn[1], across[0], across[1])))
+
+    for members, source in ((plan["relayed"], first), (plan["late"], own)):
 
         @pl.when(among(members))
         def _():
@@ -255,16 +264,20 @@
 def middle_kernel(plan, first, other, sigma, out):
     @pl.when(among(plan["mids"]))
     def _():
-        steps = [stepped(block, sigma[0], sigma[1]) for block in (first, other)]
+        steps = [stepped(block, sigma) for block in (first, other)]
         put(out, [added(*(step[part].astype(out.dtype) for step in steps)) for part in range(2)])
 
 
-def neighbour_kernel(plan, first, second, third, middle, sigma, out):
-    for members, source in ((plan["direct"], first), (plan["second_pairs"], second)):
+def neighbour_kernel(plan, first, other, second, third, middle, sigma, out):
+    for members, source in (
+        (plan["early"], first),
+        (plan["direct"], other),
+        (plan["second_pairs"], second),
+    ):
 
         @pl.when(among(members))
         def _():
-            put(out, stepped(source, sigma[0], sigma[1]))
+            put(out, stepped(source, sigma))
 
     for members, source in (
         (plan["lows"], second),
@@ -277,15 +290,12 @@
             out[...] = source[...]
 
 
-def close_kernel(plan, green, weights, out):
-    out[...] = half_energy(green, weights[1])
-
-
-def last_kernel(plan, own, near, across, weights, out):
-    size = own.shape[-1]
-    sigma = near[...] + half_energy(across, far_weight(weights))
-    sigma = sigma.astype(jnp.bfloat16)
-    put(out, stepped(own, sigma[:size], sigma[size:]))
+def close_kernel(plan, turn, green, out):
+    out[...] = around(turn[0], turn[1], green[0], green[1])
+
+
+def last_kernel(plan, own, turn, near, across, out):
+    put(out, onto(own, near[...] + around(turn[0], turn[1], across[0], across[1])))
 
 
 LIMITS = pltpu.CompilerParams(vmem_limit_bytes=VMEM_LIMIT)
@@ -302,7 +312,7 @@
         functools.partial(kernel, plan),
         out_shape=out or like(blocks[0]),
         in_specs=[IN_VMEM] * len(blocks),
-        out_specs=IN_VMEM,
+        out_specs=[IN_VMEM] * len(out) if isinstance(out, list) else IN_VMEM,
         compiler_params=LIMITS,
     )(*blocks)
 
@@ -323,7 +333,7 @@
     slabs = lax.axis_size("slab")
     everyone = range(lax.axis_size("energy"))
     size = green0.shape[-1]
-    wide = jax.ShapeDtypeStruct((2 * size, size), jnp.float32)
+    wide = jax.ShapeDtypeStruct((size, 2 * size), jnp.float32)
 
     def sent(value, flows):
         return lax.ppermute(value, "energy", plan[flows])
@@ -337,16 +347,17 @@
     first, other = sent(green0[0, 0], "first"), sent(green0[0, 0], "other")
     own, weights = loaded(far, far_weights)
     sigma = call(sigma_kernel, plan, own, swapped(own, everyone), weights)
+    near_turn, far_turn = call(turn_kernel, plan, own, weights, out=[like(own)] * 2)
     both = call(sum_kernel, plan, first, other)
     across = swapped(both, everyone)
-    near = call(near_kernel, plan, both, weights, out=wide)
-    send = call(second_kernel, plan, own, near, across, weights, other)
+    near = call(near_kernel, plan, near_turn, both, out=wide)
+    send = call(second_kernel, plan, own, far_turn, near, across, first)
     second, third = sent(send, "second"), sent(send, "third")
     middle = call(middle_kernel, plan, first, other, sigma)
-    green = call(neighbour_kernel, plan, first, second, third, middle, sigma)
+    green = call(neighbour_kernel, plan, first, other, second, third, middle, sigma)
     across = swapped(green, everyone)
-    near = call(close_kernel, plan, green, weights, out=wide)
-    out = call(last_kernel, plan, own, near, across, weights)
+    near = call(close_kernel, plan, near_turn, green, out=wide)
+    out = call(last_kernel, plan, own, far_turn, near, across)
     return out[None, None]
 
 

time: 51.2 us -> 51.1 us (level)
  waiting for transfers between devices: 35.2 us -> 34.4 us
  Pallas kernels: 4.97 us -> 5.52 us
    pallas_call x8 -> x9, Pallas kernels: 3.61 us -> 4.15 us  [call(): pl.pallas_call(functools.partial(kernel, plan), out_shape=out or like(blo...]
  transfers between devices with their start and end apart: 7 -> 7, of which waited for: 4 -> 3; matrix products, arithmetic and copies ran while one was open for 0% -> 0% of each run, Pallas kernels for 4% -> 7%
where the time goes in v1:
time: 51.1 us; the launch traced here: 50.9 us
  waiting for transfers between devices  34.4 us (67%)
  starting transfers between devices  10.8 us (21%)
  Pallas kernels  5.52 us (11%)
    ppermute x4, waiting for transfers between devices, sent(): return lax.ppermute(value, 'energy', plan[flows])  33.7 us
    ppermute x4, starting transfers between devices, sent(): return lax.ppermute(value, 'energy', plan[flows])  10.1 us
    pallas_call x9, Pallas kernels, call(): pl.pallas_call(functools.partial(kernel, plan), out_shape=out or like(blo...  4.15 us
    pallas_call x1, Pallas kernels, loaded(): pl.pallas_call(load_kernel, out_shape=[like(own), like(weights)], in_spec...  1.37 us
  transfers between devices with their start and end apart: 7, of which 3 were waited for; matrix products, arithmetic and copies ran while one was open for 0% of the time, Pallas kernels for 7%

profile of v1, /device:TPU:0, one launch (start us, length us, event | category | flops | bytes accessed | tf_op | source)
XLA Modules:
  0.0 50.9 jit_solution(10214744378832652643)
XLA Ops:
  0.0 0.7 %collective-permute-start.1 = (bf16[2,384,384]{2,1,0:T(8,128)(2,1)}, bf16[2,384,384]{2,1,0:T(8,128)(2,1)S(1)}, u32[]{:S(2)}, u32[]{:S(2)}) collective-permute-start(bf16[2,384,384]{2,1,0:T(8,128)(2,1)} %bitcast.4), channel_id=1, source_target_pairs={{28,14},{30,16},{8,22},{22,8},{29,15},{31,17},{9,23},{23,9}} | collective-permute-start | bytes 1769480 | tf_op jit(solution)/shard_map/ppermute | solution.py:339
  0.7 7.5 %collective-permute-start = (bf16[2,384,384]{2,1,0:T(8,128)(2,1)}, bf16[2,384,384]{2,1,0:T(8,128)(2,1)S(1)}, u32[]{:S(2)}, u32[]{:S(2)}) collective-permute-start(bf16[2,384,384]{2,1,0:T(8,128)(2,1)} %bitcast.5), channel_id=1, source_target_pairs={{0,14},{2,16},{6,22},{24,8},{4,18},{18,4},{1,15},{3,17},{7,23},{25... | collective-permute-start | bytes 1769480 | tf_op jit(solution)/shard_map/ppermute | solution.py:339
  8.2 0.0 collective-permute-done.1.other
  8.2 12.8 %collective-permute-done.first = bf16[2,384,384]{2,1,0:T(8,128)(2,1)S(1)} collective-permute-done((bf16[2,384,384]{2,1,0:T(8,128)(2,1)}, bf16[2,384,384]{2,1,0:T(8,128)(2,1)S(1)}, u32[]{:S(2)}, u32[]{:S(2)}) %collective-permute-start) | collective-permute-done | bytes 589856 | tf_op jit(solution)/shard_map/ppermute | solution.py:339
  21.0 0.0 collective-permute-start.2
  21.0 1.4 %load_kernel.1 = (bf16[2,384,384]{2,1,0:T(8,128)(2,1)S(1)}, bf16[3,384,384]{2,1,0:T(8,128)(2,1)S(1)}) custom-call(bf16[2,384,384]{2,1,0:T(8,128)(2,1)} %bitcast.6, bf16[3,384,384]{2,1,0:T(8,128)(2,1)} %bitcast.3), custom_call_target="tpu_custom_call" | custom-call | tf_op jit(solution)/shard_map/load_kernel/pallas_call | solution.py:321
  22.4 0.6 %collective-permute-start.5 = (bf16[2,384,384]{2,1,0:T(8,128)(2,1)S(1)}, bf16[2,384,384]{2,1,0:T(8,128)(2,1)S(1)}, u32[]{:S(2)}, u32[]{:S(2)}) collective-permute-start(bf16[2,384,384]{2,1,0:T(8,128)(2,1)S(1)} %get-tuple-element.9.own), channel_id=1, source_target_pairs={{0,1},{1,0},{2,3},{3,2},{4,5},{5,4},{6,7},{7,6},{8,9},{9,8},{10,11... | collective-permute-start | bytes 1769480 | tf_op jit(solution)/shard_map/ppermute | solution.py:343
  23.0 0.8 %shard_map.28 = (bf16[2,384,384]{2,1,0:T(8,128)(2,1)S(1)}, bf16[2,384,384]{2,1,0:T(8,128)(2,1)S(1)}) custom-call(bf16[2,384,384]{2,1,0:T(8,128)(2,1)S(1)} %get-tuple-element.9.own, bf16[3,384,384]{2,1,0:T(8,128)(2,1)S(1)} %get-tuple-element.10.weights), custom_call_target="tpu_custom_call" | custom-call | tf_op jit(solution)/shard_map/pallas_call | solution.py:311
  23.8 0.0 collective-permute-done.2.across
  23.8 0.7 %collective-permute-start.4 = (bf16[2,384,384]{2,1,0:T(8,128)(2,1)S(1)}, bf16[2,384,384]{2,1,0:T(8,128)(2,1)S(1)}, u32[]{:S(2)}, u32[]{:S(2)}) collective-permute-start(bf16[2,384,384]{2,1,0:T(8,128)(2,1)S(1)} %shard_map.31), channel_id=1, source_target_pairs={{14,28},{16,30},{15,29},{17,31}} | collective-permute-start | bytes 1769480 | tf_op jit(solution)/shard_map/ppermute | solution.py:339
  24.5 1.3 %collective-permute-start.3 = (bf16[2,384,384]{2,1,0:T(8,128)(2,1)S(1)}, bf16[2,384,384]{2,1,0:T(8,128)(2,1)S(1)}, u32[]{:S(2)}, u32[]{:S(2)}) collective-permute-start(bf16[2,384,384]{2,1,0:T(8,128)(2,1)S(1)} %shard_map.31), channel_id=1, source_target_pairs={{14,0},{16,2},{22,20},{20,6},{10,24},{8,10},{12,26},{26,12},{15,1}... | collective-permute-start | bytes 1769480 | tf_op jit(solution)/shard_map/ppermute | solution.py:339
  25.8 0.0 collective-permute-done.5.beside
  25.9 0.0 collective-permute-done.4.third
  25.9 20.8 %collective-permute-done.3.second = bf16[2,384,384]{2,1,0:T(8,128)(2,1)S(1)} collective-permute-done((bf16[2,384,384]{2,1,0:T(8,128)(2,1)S(1)}, bf16[2,384,384]{2,1,0:T(8,128)(2,1)S(1)}, u32[]{:S(2)}, u32[]{:S(2)}) %collective-permute-start.3) | collective-permute-done | bytes 589856 | tf_op jit(solution)/shard_map/ppermute | solution.py:339
  46.7 0.1 shard_map.34.green
  46.8 0.1 collective-permute-start.6
  46.9 1.2 %shard_map.35.near = f32[384,768]{1,0:T(8,128)S(1)} custom-call(bf16[2,384,384]{2,1,0:T(8,128)(2,1)S(1)} %get-tuple-element.12.turn, bf16[2,384,384]{2,1,0:T(8,128)(2,1)S(1)} %shard_map.34.green), custom_call_target="tpu_custom_call" | custom-call | tf_op jit(solution)/shard_map/pallas_call | solution.py:311
  48.1 0.8 %collective-permute-done.6.across = bf16[2,384,384]{2,1,0:T(8,128)(2,1)S(1)} collective-permute-done((bf16[2,384,384]{2,1,0:T(8,128)(2,1)S(1)}, bf16[2,384,384]{2,1,0:T(8,128)(2,1)S(1)}, u32[]{:S(2)}, u32[]{:S(2)}) %collective-permute-start.6) | collective-permute-done | bytes 589856 | tf_op jit(solution)/shard_map/ppermute | solution.py:343
  48.9 2.0 %shard_map.36 = bf16[2,384,384]{2,1,0:T(8,128)(2,1)} custom-call(bf16[2,384,384]{2,1,0:T(8,128)(2,1)S(1)} %get-tuple-element.9.own, bf16[2,384,384]{2,1,0:T(8,128)(2,1)S(1)} %get-tuple-element.11.turn, f32[384,768]{1,0:T(8,128)S(1)} %shard_map.35.near, bf16[2,384,384]{2,1,0:T(8,128)(2,1)S(1)} %collective-permute-done.6.across), custom_call_target="tpu_custom_call" | custom-call | tf_op jit(solution)/shard_map/pallas_call | solution.py:311
  (5 shorter events, 0.1 us)
Async XLA Ops:
  0.0 8.2 %collective-permute-start.1 = (bf16[2,384,384]{2,1,0:T(8,128)(2,1)}, bf16[2,384,384]{2,1,0:T(8,128)(2,1)S(1)}, u32[]{:S(2)}, u32[]{:S(2)}) collective-permute-start(bf16[2,384,384]{2,1,0:T(8,128)(2,1)} %bitcast.4), channel_id=1, source_target_pairs={{28,14},{30,16},{8,22},{22,8},{29,15},{31,17},{9,23},{23,9}} | collective-permute-start | bytes 1769480 | tf_op jit(solution)/shard_map/ppermute | solution.py:339
  0.7 20.3 %collective-permute-start = (bf16[2,384,384]{2,1,0:T(8,128)(2,1)}, bf16[2,384,384]{2,1,0:T(8,128)(2,1)S(1)}, u32[]{:S(2)}, u32[]{:S(2)}) collective-permute-start(bf16[2,384,384]{2,1,0:T(8,128)(2,1)} %bitcast.5), channel_id=1, source_target_pairs={{0,14},{2,16},{6,22},{24,8},{4,18},{18,4},{1,15},{3,17},{7,23},{25... | collective-permute-start | bytes 1769480 | tf_op jit(solution)/shard_map/ppermute | solution.py:339
  21.0 2.8 %collective-permute-start.2 = (bf16[2,384,384]{2,1,0:T(8,128)(2,1)S(1)}, bf16[2,384,384]{2,1,0:T(8,128)(2,1)S(1)}, u32[]{:S(2)}, u32[]{:S(2)}) collective-permute-start(bf16[2,384,384]{2,1,0:T(8,128)(2,1)S(1)} %shard_map.29.both), channel_id=1, source_target_pairs={{0,1},{1,0},{2,3},{3,2},{4,5},{5,4},{6,7},{7,6},{8,9},{9,8},{10,11... | collective-permute-start | bytes 1769480 | tf_op jit(solution)/shard_map/ppermute | solution.py:343
  22.4 3.4 %collective-permute-start.5 = (bf16[2,384,384]{2,1,0:T(8,128)(2,1)S(1)}, bf16[2,384,384]{2,1,0:T(8,128)(2,1)S(1)}, u32[]{:S(2)}, u32[]{:S(2)}) collective-permute-start(bf16[2,384,384]{2,1,0:T(8,128)(2,1)S(1)} %get-tuple-element.9.own), channel_id=1, source_target_pairs={{0,1},{1,0},{2,3},{3,2},{4,5},{5,4},{6,7},{7,6},{8,9},{9,8},{10,11... | collective-permute-start | bytes 1769480 | tf_op jit(solution)/shard_map/ppermute | solution.py:343
  23.8 2.1 %collective-permute-start.4 = (bf16[2,384,384]{2,1,0:T(8,128)(2,1)S(1)}, bf16[2,384,384]{2,1,0:T(8,128)(2,1)S(1)}, u32[]{:S(2)}, u32[]{:S(2)}) collective-permute-start(bf16[2,384,384]{2,1,0:T(8,128)(2,1)S(1)} %shard_map.31), channel_id=1, source_target_pairs={{14,28},{16,30},{15,29},{17,31}} | collective-permute-start | bytes 1769480 | tf_op jit(solution)/shard_map/ppermute | solution.py:339
  24.5 22.2 %collective-permute-start.3 = (bf16[2,384,384]{2,1,0:T(8,128)(2,1)S(1)}, bf16[2,384,384]{2,1,0:T(8,128)(2,1)S(1)}, u32[]{:S(2)}, u32[]{:S(2)}) collective-permute-start(bf16[2,384,384]{2,1,0:T(8,128)(2,1)S(1)} %shard_map.31), channel_id=1, source_target_pairs={{14,0},{16,2},{22,20},{20,6},{10,24},{8,10},{12,26},{26,12},{15,1}... | collective-permute-start | bytes 1769480 | tf_op jit(solution)/shard_map/ppermute | solution.py:339
  46.8 2.1 %collective-permute-start.6 = (bf16[2,384,384]{2,1,0:T(8,128)(2,1)S(1)}, bf16[2,384,384]{2,1,0:T(8,128)(2,1)S(1)}, u32[]{:S(2)}, u32[]{:S(2)}) collective-permute-start(bf16[2,384,384]{2,1,0:T(8,128)(2,1)S(1)} %shard_map.34.green), channel_id=1, source_target_pairs={{0,1},{1,0},{2,3},{3,2},{4,5},{5,4},{6,7},{7,6},{8,9},{9,8},{10,11... | collective-permute-start | bytes 1769480 | tf_op jit(solution)/shard_map/ppermute | solution.py:343
